TPU v7x, 512 devices: a whole 4x8x8 slice. The times are simulated.
512 devices in a mesh: user: 32 (over x, y_lo, core), item: 16 (over y_hi, z).
Axes of the slice: x: 4, y: 8 (y_hi: 2, y_lo: 4; y = y_hi * 4 + y_lo), z: 8, core: 2. Of those that a mesh axis runs over, the one named last changes fastest.
Arguments:
- user_emb: bfloat16 [8192, 64], P('user'), may hold values from -300 to 300
- item_emb: bfloat16 [64, 262144], P(None, ('item', 'user')), may hold values from -1.5 to 1.5
- objective_weights: float32 [4], replicated, may hold values from 0.5 to 1.5
- objective_targets: float32 [4], replicated, may hold values from 0.2 to 0.6
- objective_duals: float32 [4], replicated, may hold values from -0.5 to 0.5
- capacity_duals: float32 [262144], P('item'), may hold values from 0 to 1
- capacity: float32 [262144], P('item'), may hold values from 0.5 to 2
Outputs:
- user_soft_value: float32 [8192], P('user')
- capacity_out: float32 [262144], P('item')
- objective_out: float32 [4], replicated
All inputs are finite; a program needn't handle non-finite values.
Results may differ from a plain program's by a relative error of at most 0.0034.
Values may be sent and summed in bfloat16 or wider, within the bound.
A program may use at most 64 MiB of HBM per device.

v0:
```python
import jax
import jax.numpy as jnp
from jax import lax
from jax.sharding import PartitionSpec as P

ITERS = 2


softness_level = 2.0
dual_step = 0.5
target_step = 4.0


def per_device(
    user_emb,
    item_emb,
    objective_weights,
    objective_targets,
    objective_duals,
    capacity_duals,
    capacity,
):
    item_cols = lax.all_gather(item_emb, "user", axis=1, tiled=True)
    feature_count, item_width = item_cols.shape
    user_rows = user_emb.shape[0]
    tower_count = objective_weights.shape[0]
    embed_width = feature_count // tower_count
    block_cols = min(2048, item_width)
    block_count = item_width // block_cols
    users_total = user_rows * lax.axis_size("user")
    items_total = item_width * lax.axis_size("item")
    user_float = user_emb.astype(jnp.float32)
    tower_duals = objective_duals
    dual_now = capacity_duals
    user_soft_value = jnp.zeros((user_rows,), jnp.float32)
    for iteration in range(ITERS):
        tower_coeff = objective_weights + tower_duals
        tempered_user_rows = (user_float * jnp.repeat(tower_coeff, embed_width)[None, :]).astype(
            jnp.bfloat16
        )

        def block_logits(block_index, duals=dual_now, users=tempered_user_rows):
            block_item_vectors = lax.dynamic_slice_in_dim(
                item_cols, block_index * block_cols, block_cols, 1
            )
            block_dual_prices = lax.dynamic_slice_in_dim(
                duals, block_index * block_cols, block_cols, 0
            )
            user_item_logits = (
                jnp.dot(users, block_item_vectors, preferred_element_type=jnp.float32)
                - block_dual_prices[None, :]
            ) / softness_level
            return (user_item_logits, block_item_vectors)

        def stat_step(block_index, running):
            row_max_logit, row_exp_sum = running
            user_item_logits, unused = block_logits(block_index)
            new_max = jnp.maximum(row_max_logit, jnp.max(user_item_logits, axis=1))
            row_exp_sum = row_exp_sum * jnp.exp(row_max_logit - new_max) + jnp.sum(
                jnp.exp(user_item_logits - new_max[:, None]), axis=1
            )
            return (new_max, row_exp_sum)

        start_state = (
            jnp.full((user_rows,), -1e30, jnp.float32),
            jnp.zeros((user_rows,), jnp.float32),
        )
        row_max_logit, row_exp_sum = lax.fori_loop(0, block_count, stat_step, start_state)
        global_max = lax.pmax(row_max_logit, "item")
        row_exp_sum = lax.psum(row_exp_sum * jnp.exp(row_max_logit - global_max), "item")
        row_max_logit = global_max
        user_soft_value = softness_level * (row_max_logit + jnp.log(row_exp_sum))

        def allocate_step(block_index, running, peak=row_max_logit, totals=row_exp_sum):
            item_load, tower_sums = running
            user_item_logits, block_item_vectors = block_logits(block_index)
            exposure = jnp.exp(user_item_logits - peak[:, None]) / totals[:, None]
            item_load = lax.dynamic_update_slice_in_dim(
                item_load, jnp.sum(exposure, axis=0), block_index * block_cols, 0
            )
            tower_sums = tower_sums + lax.dot_general(
                exposure.astype(jnp.bfloat16),
                block_item_vectors,
                (((1,), (1,)), ((), ())),
                preferred_element_type=jnp.float32,
            )
            return (item_load, tower_sums)

        start_alloc = (
            jnp.zeros((item_width,), jnp.float32),
            jnp.zeros((user_rows, feature_count), jnp.float32),
        )
        item_load, tower_sums = lax.fori_loop(0, block_count, allocate_step, start_alloc)
        partial_sums = jnp.sum(
            (user_float * tower_sums).reshape(user_rows, tower_count, embed_width), axis=(0, 2)
        )
        achieved = lax.psum(partial_sums, ("user", "item")) / users_total
        load_total = lax.psum(item_load, "user")
        dual_now = jnp.maximum(
            0.0, dual_now + dual_step * (load_total * items_total / users_total - capacity)
        )
        tower_duals = tower_duals + target_step * (objective_targets - achieved)
    return (user_soft_value, dual_now, tower_duals)


def solution(mesh):
    in_specs = (P("user", None), P(None, ("item", "user")), P(), P(), P(), P("item"), P("item"))
    out_specs = (P("user"), P("item"), P())
    return jax.shard_map(
        per_device, mesh=mesh, in_specs=in_specs, out_specs=out_specs, check_vma=False
    )
```

profile of v0, /device:TPU:1, one launch (start us, length us, event | category | flops | bytes accessed | tf_op | source)
XLA Modules:
  0.0 1062.5 jit_solution(14100818702496083265)
XLA Ops:
  9.8 68.6 %all-gather.2.cloned.1.call-done = bf16[64,16384]{1,0:T(8,128)(2,1)} async-done(((bf16[64,512]{1,0:T(8,128)(2,1)}), bf16[64,16384]{1,0:T(8,128)(2,1)}) %all-gather.2.cloned.1.call-update) | async-done | bytes 2097168 | tf_op jit(solution)/shard_map/all_gather | solution.py:23
  78.4 20.8 %while.64 = (s32[]{:T(128)}, f32[256]{0:T(256)S(1)}, f32[256]{0:T(256)S(1)}, bf16[64,16384]{1,0:T(8,128)(2,1)}, bf16[256,64]{1,0:T(8,128)(2,1)S(1)}, /*index=5*/...) while((s32[]{:T(128)}, f32[256]{0:T(256)S(1)}, f32[256]{0:T(256)S(1)}, ...), condition=%wide.region_3.0_spmd.clone, body=%wide.region_0.0_spmd.clone.sunk | while | flops 69731592 | bytes 4527270 | solution.py:68
  79.1 1.5 fusion.60
  81.7 1.5 fusion.60
  84.3 1.5 fusion.60
  86.9 1.5 fusion.60
  89.5 1.5 fusion.60
  92.1 1.5 fusion.60
  94.7 1.5 fusion.60
  97.3 1.5 fusion.60
  99.2 46.5 %pmax.14 = f32[256]{0:T(256)S(1)} all-reduce(f32[256]{0:T(256)S(1)} %get-tuple-element.503), channel_id=1, replica_groups=mesh['user'=32,'item'=16] {'item'}, use_global_device_ids=true, to_apply=%region_4.0 | all-reduce | flops 256 | bytes 2048 | tf_op jit(solution)/shard_map/pmax | solution.py:69
  145.7 39.7 %psum.42 = f32[256]{0:T(256)S(1)} all-reduce(f32[256]{0:T(256)S(1)} %exponential_multiply_fusion.1), channel_id=1, replica_groups=mesh['user'=32,'item'=16] {'item'}, use_global_device_ids=true, to_apply=%region_5.0 | all-reduce | flops 256 | bytes 2048 | tf_op jit(solution)/shard_map/psum | solution.py:70
  185.5 33.1 %while.65 = (s32[]{:T(128)}, f32[16384]{0:T(1024)S(1)}, f32[256,64]{0,1:T(8,128)S(1)}, bf16[64,16384]{1,0:T(8,128)(2,1)}, bf16[256,64]{1,0:T(8,128)(2,1)S(1)}, /...) while((s32[]{:T(128)}, f32[16384]{0:T(1024)S(1)}, ...), condition=%wide.region_8.0_spmd.clone, body=%wide.region_6.0_spmd.clone.sunk | while | flops 137394176 | bytes 2836669 | solution.py:93
  186.2 1.7 fusion.66
  187.9 1.4 convolution_add_fusion.4
  190.4 1.7 fusion.66
  194.5 1.7 fusion.66
  198.6 1.7 fusion.66
  202.8 1.7 fusion.66
  206.9 1.7 fusion.66
  211.0 1.7 fusion.66
  215.2 1.7 fusion.66
  218.9 108.1 %psum.43 = f32[4]{0:T(128)S(1)} all-reduce(f32[4]{0:T(128)S(1)} %reduce_sum.86), channel_id=1, replica_groups=mesh['user'=32,'item'=16] {'user','item'}, use_global_device_ids=true, to_apply=%region_12.13 | all-reduce | flops 4 | bytes 32 | tf_op jit(solution)/shard_map/psum | solution.py:97
  327.4 242.0 %all-reduce.3.cloned.1.call-done = f32[16384]{0:T(1024)} async-done(((f32[16384]{0:T(1024)}), f32[16384]{0:T(1024)}) %all-reduce.3.cloned.1.call-update) | async-done | bytes 65552 | tf_op jit(solution)/shard_map/psum | solution.py:98
  570.3 15.4 %while.66 = (s32[]{:T(128)}, f32[256]{0:T(256)S(1)}, f32[256]{0:T(256)S(1)}, bf16[64,16384]{1,0:T(8,128)(2,1)}, bf16[256,64]{1,0:T(8,128)(2,1)S(1)}, /*index=5*/...) while((s32[]{:T(128)}, f32[256]{0:T(256)S(1)}, f32[256]{0:T(256)S(1)}, ...), condition=%wide.region_16.0_spmd.clone, body=%wide.region_13.16_spmd.clone.sunk | while | flops 69731592 | bytes 4527270 | solution.py:68
  570.3 1.5 fusion.68
  572.3 1.5 fusion.68
  574.2 1.5 fusion.68
  576.1 1.5 fusion.68
  578.0 1.5 fusion.68
  580.0 1.5 fusion.68
  581.9 1.5 fusion.68
  583.8 1.5 fusion.68
  585.7 46.0 %pmax.15 = f32[256]{0:T(256)S(1)} all-reduce(f32[256]{0:T(256)S(1)} %get-tuple-element.507), channel_id=1, replica_groups=mesh['user'=32,'item'=16] {'item'}, use_global_device_ids=true, to_apply=%region_17.0 | all-reduce | flops 256 | bytes 2048 | tf_op jit(solution)/shard_map/pmax | solution.py:69
  631.7 39.3 %psum.45 = f32[256]{0:T(256)S(1)} all-reduce(f32[256]{0:T(256)S(1)} %exponential_multiply_fusion), channel_id=1, replica_groups=mesh['user'=32,'item'=16] {'item'}, use_global_device_ids=true, to_apply=%region_18.19 | all-reduce | flops 256 | bytes 2048 | tf_op jit(solution)/shard_map/psum | solution.py:70
  671.0 27.6 %while.67 = (s32[]{:T(128)}, f32[16384]{0:T(1024)S(1)}, f32[256,64]{0,1:T(8,128)S(1)}, bf16[64,16384]{1,0:T(8,128)(2,1)}, bf16[256,64]{1,0:T(8,128)(2,1)S(1)}, /...) while((s32[]{:T(128)}, f32[16384]{0:T(1024)S(1)}, ...), condition=%wide.region_21.0_spmd.clone, body=%wide.region_19.21_spmd.clone.sunk | while | flops 137394176 | bytes 2836669 | solution.py:93
  671.0 1.7 fusion.74
  672.7 1.4 convolution_add_fusion.5
  674.5 1.7 fusion.74
  677.9 1.7 fusion.74
  681.4 1.7 fusion.74
  684.8 1.7 fusion.74
  688.3 1.7 fusion.74
  691.7 1.7 fusion.74
  695.2 1.7 fusion.74
  699.5 112.6 %psum.47 = f32[4]{0:T(128)S(1)} all-reduce(f32[4]{0:T(128)S(1)} %reduce_sum.89), channel_id=1, replica_groups=mesh['user'=32,'item'=16] {'user','item'}, use_global_device_ids=true, to_apply=%region_25.26 | all-reduce | flops 4 | bytes 32 | tf_op jit(solution)/shard_map/psum | solution.py:97
  812.7 241.8 %all-reduce.5.cloned.1.call-done = f32[16384]{0:T(1024)} async-done(((f32[16384]{0:T(1024)}), f32[16384]{0:T(1024)}) %all-reduce.5.cloned.1.call-update) | async-done | bytes 65552 | tf_op jit(solution)/shard_map/psum | solution.py:98
  1054.5 1.5 add_maximum_fusion
  (175 shorter events, 48.2 us)
Async XLA Ops:
  7.2 71.2 %all-gather.2.cloned.1.call-start = ((), (), s32[]{:S(2)}) async-start(), calls=%async_computation | async-start | bytes 2162688 | tf_op jit(solution)/shard_map/all_gather | solution.py:23
  7.9 561.5 %all-reduce.3.cloned.1.call-start = ((), (), s32[]{:S(2)}) async-start(), calls=%async_computation.1 | async-start | bytes 131072 | tf_op jit(solution)/shard_map/psum | solution.py:98
  185.4 33.1 %copy-start = (bf16[256,64]{0,1:T(8,128)(2,1)S(1)}, bf16[256,64]{0,1:T(8,128)(2,1)}, u32[]{:S(2)}) copy-start(bf16[256,64]{0,1:T(8,128)(2,1)} %param.15) | copy-start | bytes 98308
  185.4 141.6 %copy-start.4 = (f32[4]{0:T(128)S(1)}, f32[4]{0:T(128)}, u32[]{:S(2)}) copy-start(f32[4]{0:T(128)} %param.19) | copy-start | bytes 52
  185.4 141.5 %copy-start.5 = (f32[4]{0:T(128)S(1)}, f32[4]{0:T(128)}, u32[]{:S(2)}) copy-start(f32[4]{0:T(128)} %param.18) | copy-start | bytes 52
  185.5 141.5 %copy-start.6 = (f32[4]{0:T(128)S(1)}, f32[4]{0:T(128)}, u32[]{:S(2)}) copy-start(f32[4]{0:T(128)} %param.17) | copy-start | bytes 52
  185.5 383.9 %copy-start.3 = (f32[16384]{0:T(1024)S(1)}, f32[16384]{0:T(1024)}, u32[]{:S(2)}) copy-start(f32[16384]{0:T(1024)} %param.21) | copy-start | bytes 196612
  218.6 108.6 %copy-start.1 = (f32[16384]{0:T(1024)}, f32[16384]{0:T(1024)S(1)}, u32[]{:S(2)}) copy-start(f32[16384]{0:T(1024)S(1)} %get-tuple-element.506) | copy-start | bytes 196612
  327.2 727.3 %all-reduce.5.cloned.1.call-start = ((), (), s32[]{:S(2)}) async-start(), calls=%async_computation.2 | async-start | bytes 131072 | tf_op jit(solution)/shard_map/psum | solution.py:98
  698.6 113.5 %copy-start.2 = (f32[16384]{0:T(1024)}, f32[16384]{0:T(1024)S(1)}, u32[]{:S(2)}) copy-start(f32[16384]{0:T(1024)S(1)} %get-tuple-element.509) | copy-start | bytes 196612
Sparse Core Ops, SparseCore 0:
  10.1 68.1 all-gather.1
  327.3 242.0 all-reduce.2
  812.3 242.1 all-reduce.4
where the time goes:
time: 1070 us; the launch traced here: 1060 us
  waiting for transfers between devices  553 us (52%)
  blocking collectives  392 us (37%)
  matrix products  73.1 us (7%)
  local copies, waits for them, and re-layouts  17.4 us (2%)
  between operations  13.9 us (1%)
  other arithmetic  11.7 us (1%)
    psum x2, waiting for transfers between devices, per_device(): load_total = lax.psum(item_load, 'user')  484 us
    psum x2, blocking collectives, per_device(): achieved = lax.psum(partial_sums, ('user', 'item')) / users_total  221 us
    pmax x2, blocking collectives, per_device(): global_max = lax.pmax(row_max_logit, 'item')  92.5 us
    psum x2, blocking collectives, per_device(): lax.psum(row_exp_sum * jnp.exp(row_max_logit - global_max), 'item')  79 us
    all_gather x1, waiting for transfers between devices, per_device(): item_cols = lax.all_gather(item_emb, 'user', axis=1, tiled=True)  68.6 us
    dot_general x32, matrix products, block_logits(): jnp.dot(users, block_item_vectors, preferred_element_type=jnp.float32)  50.5 us
    dot_general x16, matrix products, allocate_step(): lax.dot_general(exposure.astype(jnp.bfloat16), block_item_vectors, (((1,)...  22.6 us
  transfers between devices with their start and end apart: 3, of which 3 were waited for; matrix products, arithmetic and copies ran while one was open for 0% of the time, Pallas kernels for 0%

commit v1 on v0

v1 whole, which is shorter than its diff:
```python
import functools
from types import SimpleNamespace

import jax
import jax.numpy as jnp
from jax import lax
from jax.experimental import pallas as pl
from jax.experimental.pallas import tpu as pltpu
from jax.sharding import PartitionSpec as P

ITERS = 2
TAU = 2.0
DUAL_STEP = 0.5
TARGET_STEP = 4.0
MESH = pl.DeviceIdType.MESH

SLICE = SimpleNamespace(X=4, YL=4, C=2, YH=2, Z=8)

F32 = jnp.float32
BF16 = jnp.bfloat16
UD = 256
IB = 512
KD = 128


def kernel(
    g,
    user_ref, item_ref, ow_ref, ot_ref, od_ref, duals_ref, cap_ref,
    soft_out, cap_out, obj_out,
    upk, iaug, uaug, zbuf, ebuf, macc, sacc, tacc, wl, lam, capl,
    yms, yn, zms, zn, xload, xach, agbuf,
    gi_s, gi_r, gu_s, gu_r,
    yms_s, yms_r, yn_s, yn_r, zms_s, zms_r, zn_s, zn_r,
    xl_s, xl_r, xa_s, xa_r, ag_s, ag_r,
):
    X, YL, C, YH, Z = g.X, g.YL, g.C, g.YH, g.Z
    Y, XC = YL * YH, X * C
    NU = UD * YL
    NC = NU // 128
    users_total = UD * X * YL * C
    items_total = IB * X * YL * C * YH * Z
    ui = lax.axis_index("user")
    ii = lax.axis_index("item")
    c = ui % C
    yl = (ui // C) % YL
    x = ui // (C * YL)
    yh = ii // Z
    z = ii % Z
    y = yh * YL + yl
    xc = x * C + c

    def dev(x_, y_, c_, z_):
        return ((x_ * YL + y_ % YL) * C + c_, (y_ // YL) * Z + z_)

    ypeers = [dev(x, (y + d) % Y, c, z) for d in range(1, Y)]
    zpeers = [dev(x, y, c, (z + d) % Z) for d in range(1, Z)]
    xpeers = [
        dev((x + dx) % X, y, (c + dc) % C, z)
        for dx in range(X) for dc in range(C) if (dx, dc) != (0, 0)
    ]
    lpeers = [dev(x, yh * YL + (yl + d) % YL, c, z) for d in range(1, YL)]

    barrier = pltpu.get_barrier_semaphore()
    peers = ypeers + zpeers + xpeers
    for p in peers:
        pl.semaphore_signal(barrier, inc=1, device_id=p, device_id_type=MESH)

    up = jnp.concatenate(
        [user_ref[0:128, :].astype(F32), user_ref[128:256, :].astype(F32)], axis=1
    ).astype(BF16)
    upk[yl] = up
    iaug[xc, 0:64, :] = item_ref[...]
    for b in range(XC):
        iaug[b, 64:128, :] = jnp.zeros((64, IB), BF16)
    RX = 4 * C
    for xx in range(X):
        base = pl.multiple_of((xx * YL + yl) * RX, RX)
        lam[xx * RX:(xx + 1) * RX, :] = duals_ref[pl.ds(base, RX), :]
        capl[xx * RX:(xx + 1) * RX, :] = cap_ref[pl.ds(base, RX), :]

    pl.semaphore_wait(barrier, len(peers))

    def copies(src, dst, ss, rs, targets):
        out = [
            pltpu.make_async_remote_copy(
                src_ref=src, dst_ref=dst, send_sem=ss.at[k], recv_sem=rs.at[k],
                device_id=t, device_id_type=MESH,
            )
            for k, t in enumerate(targets)
        ]
        for q in out:
            q.start()
        return out

    pending = []
    gu = copies(upk.at[yl], upk.at[yl], gu_s, gu_r, lpeers)
    gi = copies(item_ref, iaug.at[xc, pl.ds(0, 64), :], gi_s, gi_r, xpeers)
    pending += gu + gi

    lane = lax.broadcasted_iota(jnp.int32, (1, 128), 1)
    tower = (lane % 64) // 16
    lane128 = lax.broadcasted_iota(jnp.int32, (128, 128), 1)
    sub16 = lax.broadcasted_iota(jnp.int32, (16, 128), 0)

    def by_tower(vals):
        out = jnp.zeros((1, 128), F32)
        for k in range(4):
            out = jnp.where(tower == k, vals[k], out)
        return out

    owv = by_tower([ow_ref[k] for k in range(4)])
    otv = by_tower([ot_ref[k] for k in range(4)])
    mu = by_tower([od_ref[k] for k in range(4)])

    def put_lambda():
        lv = lam[...]
        hi = lv.astype(BF16).astype(F32)
        r1 = lv - hi
        mid = r1.astype(BF16).astype(F32)
        lo = (r1 - mid).astype(BF16).astype(F32)
        for r in range(4 * XC):
            t = jnp.where(
                sub16 == 0, hi[r:r + 1, :],
                jnp.where(sub16 == 1, mid[r:r + 1, :],
                          jnp.where(sub16 == 2, lo[r:r + 1, :], 0.0)))
            iaug[r // 4, 64:80, (r % 4) * 128:(r % 4 + 1) * 128] = t.astype(BF16)

    put_lambda()
    for q in gu:
        q.wait_recv()

    def put_users(muv):
        coef = owv + muv

        def body(b, carry):
            pk = upk[b].astype(F32)
            sc = (pk * coef).astype(BF16).astype(F32) * (1.0 / TAU)
            for h in range(2):
                t = sc if h == 0 else pltpu.roll(sc, 64, 1)
                t = jnp.where(lane128 < 64, t, jnp.where(lane128 < 67, -1.0 / TAU, 0.0))
                uaug[pl.ds(pl.multiple_of(b * 256 + h * 128, 128), 128), :] = t.astype(BF16)
            return carry

        lax.fori_loop(0, YL, body, 0)

    put_users(mu)
    for q in gi:
        q.wait_recv()

    NUB = NU // 256

    for it in range(ITERS):
        macc[...] = jnp.full((NU, 128), -3.0e38, F32)

        def pass1(t, carry):
            b, ub = t // NUB, t % NUB
            rows = pl.ds(pl.multiple_of(ub * 256, 256), 256)
            zt = jnp.dot(uaug[rows, :], iaug[b], preferred_element_type=F32)
            zbuf[b, rows, :] = zt
            m = jnp.maximum(jnp.maximum(zt[:, 0:128], zt[:, 128:256]),
                            jnp.maximum(zt[:, 256:384], zt[:, 384:512]))
            macc[rows, :] = jnp.maximum(macc[rows, :], m)
            return carry

        lax.fori_loop(0, XC * NUB, pass1, 0)
        for q in range(NC):
            rows = slice(q * 128, (q + 1) * 128)
            m = jnp.max(macc[rows, :], axis=1, keepdims=True)
            macc[rows, :] = jnp.broadcast_to(m, (128, 128))
        sacc[...] = jnp.zeros((NU, 128), F32)
        tacc[...] = jnp.zeros((NU, 128), F32)

        def pass2(t, carry):
            b, ub = t // NUB, t % NUB
            rows = pl.ds(pl.multiple_of(ub * 256, 256), 256)
            mb = macc[rows, :]
            parts = [jnp.exp(zbuf[b, rows, k * 128:(k + 1) * 128] - mb) for k in range(4)]
            sacc[rows, :] += (parts[0] + parts[1]) + (parts[2] + parts[3])
            e16 = jnp.concatenate(parts, axis=1).astype(BF16)
            ebuf[b, rows, :] = e16
            tacc[rows, :] += lax.dot_general(
                e16, iaug[b], (((1,), (1,)), ((), ())), preferred_element_type=F32)
            return carry

        lax.fori_loop(0, XC * NUB, pass2, 0)

        def stats(q, carry):
            rows = pl.ds(pl.multiple_of(q * 128, 128), 128)
            pk = upk[q // 2].astype(F32)
            uf = jnp.where(q % 2 == 0, pk, pltpu.roll(pk, 64, 1))
            p = jnp.where(lane128 < 64, uf * tacc[rows, :], macc[rows, :])
            pt = p.T
            st = sacc[rows, :].T
            one = pl.ds(q, 1)
            yms[it, y, 0, one, :] = pt[64:65, :]
            yms[it, y, 1, one, :] = jnp.sum(st, axis=0, keepdims=True)
            for k in range(4):
                yn[it, y, k, one, :] = jnp.sum(pt[16 * k:16 * k + 16, :], axis=0, keepdims=True)
            return carry

        lax.fori_loop(0, NC, stats, 0)

        cy_ms = copies(yms.at[it, y], yms.at[it, y], yms_s.at[it], yms_r.at[it], ypeers)
        cy_n = copies(yn.at[it, y], yn.at[it, y], yn_s.at[it], yn_r.at[it], ypeers)
        m_loc = yms[it, y, 0]
        for q in cy_ms:
            q.wait_recv()
        ms = yms[it]
        my = jnp.max(ms[:, 0], axis=0)
        fy = jnp.exp(ms[:, 0] - my[None])
        zms[it, z, 0] = my
        zms[it, z, 1] = jnp.sum(ms[:, 1] * fy, axis=0)
        cz_ms = copies(zms.at[it, z], zms.at[it, z], zms_s.at[it], zms_r.at[it], zpeers)
        for q in cy_n:
            q.wait_recv()
        nv = yn[it]
        for k in range(4):
            zn[it, z, k] = jnp.sum(nv[:, k] * fy, axis=0)
        cz_n = copies(zn.at[it, z], zn.at[it, z], zn_s.at[it], zn_r.at[it], zpeers)
        for q in cz_ms:
            q.wait_recv()
        ms = zms[it]
        mg = jnp.max(ms[:, 0], axis=0)
        fz = jnp.exp(ms[:, 0] - mg[None])
        sg = jnp.sum(ms[:, 1] * fz, axis=0)
        inv = 1.0 / sg
        w = jnp.exp(m_loc - mg) * inv
        if it == ITERS - 1:
            macc[0:NC, :] = TAU * (mg + jnp.log(sg))
            soft_out[...] = macc[pl.ds(yl * 2, 2), :]
        whi = w.astype(BF16).astype(F32)
        r1 = w - whi
        wmid = r1.astype(BF16).astype(F32)
        wlo = (r1 - wmid).astype(BF16).astype(F32)
        for q in range(NC):
            t = jnp.where(
                sub16 == 0, whi[q:q + 1, :],
                jnp.where(sub16 == 1, wmid[q:q + 1, :],
                          jnp.where(sub16 == 2, wlo[q:q + 1, :], 0.0)))
            wl[:, q * 128:(q + 1) * 128] = t.astype(BF16)
        for b in range(XC):
            acc = jnp.dot(wl[...], ebuf[b], preferred_element_type=F32)
            row = acc[0:1, :] + acc[1:2, :] + acc[2:3, :]
            for k in range(4):
                xload[it, xc, 4 * b + k:4 * b + k + 1, :] = row[:, k * 128:(k + 1) * 128]
        cx_l = copies(xload.at[it, xc], xload.at[it, xc], xl_s.at[it], xl_r.at[it], xpeers)
        for q in cz_n:
            q.wait_recv()
        nv = zn[it]
        xach[it, xc] = jnp.zeros((8, 128), F32)
        for k in range(4):
            t = jnp.sum(nv[:, k] * fz, axis=0) * inv
            xach[it, xc, k:k + 1, :] = jnp.sum(t, axis=0, keepdims=True)
        cx_a = copies(xach.at[it, xc], xach.at[it, xc], xa_s.at[it], xa_r.at[it], xpeers)
        for q in cx_a:
            q.wait_recv()
        ach = jnp.sum(jnp.sum(xach[it], axis=0), axis=1, keepdims=True) / users_total
        achv = by_tower([ach[k:k + 1, :] for k in range(4)])
        mu = mu + TARGET_STEP * (otv - achv)
        if it < ITERS - 1:
            put_users(mu)
        for q in cx_l:
            q.wait_recv()
        load = jnp.sum(xload[it], axis=0)
        lam[...] = jnp.maximum(
            0.0, lam[...] + DUAL_STEP * (load * (items_total / users_total) - capl[...]))
        if it < ITERS - 1:
            put_lambda()
        pending += cy_ms + cy_n + cz_ms + cz_n + cx_l + cx_a

    agbuf[yl] = lam[...]
    if YL > 1:
        ca = copies(agbuf.at[yl], agbuf.at[yl], ag_s, ag_r, lpeers)
        for q in ca:
            q.wait_recv()
        pending += ca
    for l in range(YL):
        for xx in range(X):
            cap_out[(xx * YL + l) * RX:(xx * YL + l + 1) * RX, :] = agbuf[l, xx * RX:(xx + 1) * RX, :]
    for k in range(4):
        obj_out[k] = jnp.max(jnp.where(lane == 16 * k, mu, -3.0e38))
    for q in pending:
        q.wait_send()


def per_device(g, user_emb, item_emb, ow, ot, od, duals, cap):
    X, YL, C, YH, Z = g.X, g.YL, g.C, g.YH, g.Z
    Y, XC, NU = YL * YH, X * C, UD * YL
    NC = NU // 128
    rows = IB * X * YL * C // 128
    vm = pl.BlockSpec(memory_space=pltpu.VMEM)
    sm = pl.BlockSpec(memory_space=pltpu.SMEM)
    dma = pltpu.SemaphoreType.DMA
    V = pltpu.VMEM
    nl = max(YL - 1, 1)
    soft, capo, obj = pl.pallas_call(
        functools.partial(kernel, g),
        out_shape=(
            jax.ShapeDtypeStruct((UD // 128, 128), F32),
            jax.ShapeDtypeStruct((rows, 128), F32),
            jax.ShapeDtypeStruct((4,), F32),
        ),
        in_specs=[vm, vm, sm, sm, sm, vm, vm],
        out_specs=(vm, vm, sm),
        scratch_shapes=[
            V((YL, 128, 128), BF16),
            V((XC, KD, IB), BF16),
            V((NU, KD), BF16),
            V((XC, NU, IB), F32),
            V((XC, NU, IB), BF16),
            V((NU, 128), F32),
            V((NU, 128), F32),
            V((NU, 128), F32),
            V((16, NU), BF16),
            V((4 * XC, 128), F32),
            V((4 * XC, 128), F32),
            V((ITERS, Y, 2, NC, 128), F32),
            V((ITERS, Y, 4, NC, 128), F32),
            V((ITERS, Z, 2, NC, 128), F32),
            V((ITERS, Z, 4, NC, 128), F32),
            V((ITERS, XC, 4 * XC, 128), F32),
            V((ITERS, XC, 8, 128), F32),
            V((YL, 4 * XC, 128), F32),
            dma((XC - 1,)), dma((XC - 1,)), dma((nl,)), dma((nl,)),
            dma((ITERS, Y - 1)), dma((ITERS, Y - 1)), dma((ITERS, Y - 1)), dma((ITERS, Y - 1)),
            dma((ITERS, Z - 1)), dma((ITERS, Z - 1)), dma((ITERS, Z - 1)), dma((ITERS, Z - 1)),
            dma((ITERS, XC - 1)), dma((ITERS, XC - 1)), dma((ITERS, XC - 1)), dma((ITERS, XC - 1)),
            dma((nl,)), dma((nl,)),
        ],
        compiler_params=pltpu.CompilerParams(
            collective_id=0, has_side_effects=True, vmem_limit_bytes=60 * 1024 * 1024),
        name="dual_ascent",
    )(user_emb, item_emb, ow, ot, od, duals.reshape(rows, 128), cap.reshape(rows, 128))
    return soft.reshape(UD), capo.reshape(rows * 128), obj


def solution(mesh, g=SLICE):
    in_specs = (P("user", None), P(None, ("item", "user")), P(), P(), P(), P("item"), P("item"))
    out_specs = (P("user"), P("item"), P())
    return jax.shard_map(
        functools.partial(per_device, g), mesh=mesh, in_specs=in_specs, out_specs=out_specs,
        check_vma=False,
    )
```

time: 1070 us -> 102 us (0.10)
  waiting for transfers between devices: 553 us -> 0 us
  blocking collectives: 392 us -> 0 us
  Pallas kernels: 0 us -> 96.1 us
  matrix products: 73.1 us -> 0 us
  between operations: 13.9 us -> 0.65 us
  local copies, waits for them, and re-layouts: 17.4 us -> 4.72 us
  other arithmetic: 11.7 us -> 0 us
    psum x2 -> x0, waiting for transfers between devices: 484 us -> none  [per_device(): load_total = lax.psum(item_load, 'user')]
    psum x4 -> x0, blocking collectives: 300 us -> none  [the longest x2 221 us: per_device(): achieved = lax.psum(partial_sums, ('user', 'item')) / users_total]
    pallas_call x0 -> x1, Pallas kernels: none -> 96.1 us  [per_device(): pl.pallas_call(functools.partial(kernel, g), out_shape=(jax.ShapeDtypeStr...]
    pmax x2 -> x0, blocking collectives: 92.5 us -> none  [per_device(): global_max = lax.pmax(row_max_logit, 'item')]
    dot_general x48 -> x0, matrix products: 73.1 us -> none  [the longest x32 50.5 us: block_logits(): jnp.dot(users, block_item_vectors, preferred_element_type=jnp.float32)]
    all_gather x1 -> x0, waiting for transfers between devices: 68.6 us -> none  [per_device(): item_cols = lax.all_gather(item_emb, 'user', axis=1, tiled=True)]
    dynamic_slice x32 -> x0, local copies, waits for them, and re-layouts: 11.4 us -> none  [block_logits(): lax.dynamic_slice_in_dim(duals, block_index * block_cols, block_cols, 0)]
  transfers between devices with their start and end apart: 3 -> 0, of which waited for: 3 -> 0; matrix products, arithmetic and copies ran while one was open for 0% -> 0% of each run, Pallas kernels for 0% -> 0%
where the time goes in v1:
time: 102 us; the launch traced here: 101 us
  Pallas kernels  96.1 us (94%)
  local copies, waits for them, and re-layouts  4.72 us (5%)
    pallas_call x1, Pallas kernels, per_device(): pl.pallas_call(functools.partial(kernel, g), out_shape=(jax.ShapeDtypeStr...  96.1 us
    unnamed x8, local copies, waits for them, and re-layouts  4.72 us

profile of v1, /device:TPU:1, one launch (start us, length us, event | category | flops | bytes accessed | tf_op | source)
XLA Modules:
  0.0 101.4 jit_solution(8506234292345393858)
XLA Ops:
  0.6 1.5 %copy.10.user_ref = bf16[256,64]{1,0:T(8,128)(2,1)} copy(bf16[256,64]{0,1:T(8,128)(2,1)} %param.7) | data formatting | bytes 65536 | tf_op args[0]
  2.1 96.1 %dual_ascent.1 = (f32[2,128]{1,0:T(2,128)}, f32[128,128]{1,0:T(8,128)}, f32[4]{0:T(128)}) custom-call(bf16[256,64]{1,0:T(8,128)(2,1)} %copy.10.user_ref, bf16[64,512]{1,0:T(8,128)(2,1)} %item_ref.1, f32[4]{0:T(128)} %ow_ref.1, f32[4]{0:T(128)} %ot_ref.1, f32[4]{0:T(128)} %od_ref.1, f32[128,128]{1,0:T(8,128)} %bitcast.5, f32[128,128]{1,0:T(8,128)} %bitcast.6), custom_call_target="tpu_custom_call" | custom-call | tf_op jit(solution)/shard_map/dual_ascent/pallas_call | solution.py:296
  98.2 0.0 copy-start
  98.2 0.7 copy-done
  98.9 0.6 copy.14
  99.4 0.0 copy-start.1
  99.4 1.5 %copy.15 = f32[16384]{0:T(1024)} copy(f32[16384]{0:T(1024)} %bitcast.4) | data formatting | bytes 131072
  100.9 0.0 copy-done.1
  100.9 0.5 copy.16
Async XLA Ops:
  98.2 0.7 copy-start
  99.4 1.5 %copy-start.1 = (f32[4]{0:T(128)S(1)}, f32[4]{0:T(128)}, u32[]{:S(2)}) copy-start(f32[4]{0:T(128)} %get-tuple-element.14) | copy-start | bytes 52

commit v2 on v1

v2 whole, which is shorter than its diff:
```python
import functools
from types import SimpleNamespace

import jax
import jax.numpy as jnp
from jax import lax
from jax.experimental import pallas as pl
from jax.experimental.pallas import tpu as pltpu
from jax.sharding import PartitionSpec as P

ITERS = 2
TAU = 2.0
DUAL_STEP = 0.5
TARGET_STEP = 4.0
MESH = pl.DeviceIdType.MESH

SLICE = SimpleNamespace(X=4, YL=4, C=2, YH=2, Z=8)

F32 = jnp.float32
BF16 = jnp.bfloat16
UD = 256
IB = 512
KD = 128


def kernel(
    g,
    user_hbm, item_hbm, duals_hbm, cap_hbm, ow_ref, ot_ref, od_ref,
    soft_out, cap_out, obj_out,
    ut, uraw, iaug, uaug, zbuf, ebuf, macc, tacc, st, wl, lam, capl,
    yll, yn, zll, zn, xload, xach, agbuf,
    in_s, gi_s, gi_r, gu_s, gu_r,
    yl_s, yl_r, yn_s, yn_r, zl_s, zl_r, zn_s, zn_r,
    xl_s, xl_r, xa_s, xa_r, ag_s, ag_r,
):
    X, YL, C, YH, Z = g.X, g.YL, g.C, g.YH, g.Z
    Y, XC = YL * YH, X * C
    NU = UD * YL
    NC = NU // 128
    users_total = UD * X * YL * C
    items_total = IB * X * YL * C * YH * Z
    ui = lax.axis_index("user")
    ii = lax.axis_index("item")
    c = ui % C
    yl = (ui // C) % YL
    x = ui // (C * YL)
    yh = ii // Z
    z = ii % Z
    y = yh * YL + yl
    xc = x * C + c

    def dev(x_, y_, c_, z_):
        return ((x_ * YL + y_ % YL) * C + c_, (y_ // YL) * Z + z_)

    def far_first(n):
        return sorted(range(1, n), key=lambda d: -min(d, n - d))

    near = far_first(X)[::-1]
    ypeers = [dev(x, (y + d) % Y, c, z) for d in far_first(Y)]
    zpeers = [dev(x, y, c, (z + d) % Z) for d in far_first(Z)]
    xpeers = [
        dev((x + dx) % X, y, (c + dc) % C, z)
        for dx in far_first(X) + [0] for dc in range(C) if (dx, dc) != (0, 0)
    ]
    lpeers = [dev(x, yh * YL + (yl + d) % YL, c, z) for d in range(1, YL)]

    barrier = pltpu.get_barrier_semaphore()
    peers = ypeers + zpeers + xpeers
    for p in peers:
        pl.semaphore_signal(barrier, inc=1, device_id=p, device_id_type=MESH)

    own_items = iaug.at[xc, pl.ds(0, 64), :]
    local = [
        pltpu.make_async_copy(user_hbm, ut.at[yl], in_s.at[0]),
        pltpu.make_async_copy(item_hbm, own_items, in_s.at[1]),
    ]
    RX = 4 * C
    for xx in range(X):
        rows = pl.ds(pl.multiple_of((xx * YL + yl) * RX, RX), RX)
        mine = pl.ds(xx * RX, RX)
        local.append(pltpu.make_async_copy(duals_hbm.at[rows], lam.at[mine], in_s.at[2 + 2 * xx]))
        local.append(pltpu.make_async_copy(cap_hbm.at[rows], capl.at[mine], in_s.at[3 + 2 * xx]))
    for q in local:
        q.start()
    for b in range(XC):
        iaug[b, 64:128, :] = jnp.zeros((64, IB), BF16)
    for q in local:
        q.wait()

    def send(src, dst, ss, rs, target):
        q = pltpu.make_async_remote_copy(
            src_ref=src, dst_ref=dst, send_sem=ss, recv_sem=rs,
            device_id=target, device_id_type=MESH)
        q.start()
        return q

    def copies(src, dst, ss, rs, targets):
        return [send(src, dst, ss.at[k], rs.at[k], t) for k, t in enumerate(targets)]

    lane = lax.broadcasted_iota(jnp.int32, (1, 128), 1)
    tower = lane // 16
    lane128 = lax.broadcasted_iota(jnp.int32, (128, 128), 1)
    sub16 = lax.broadcasted_iota(jnp.int32, (16, 128), 0)
    sub64 = lax.broadcasted_iota(jnp.int32, (64, 128), 0)

    def by_tower(vals, rest):
        out = jnp.full((1, 128), rest, F32)
        for k in range(4):
            out = jnp.where(tower == k, vals[k], out)
        return out

    owv = by_tower([ow_ref[k] for k in range(4)], 1.0)
    otv = by_tower([ot_ref[k] for k in range(4)], 0.0)
    mu = by_tower([od_ref[k] for k in range(4)], 0.0)

    def put_lambda():
        lv = lam[...]
        hi = lv.astype(BF16).astype(F32)
        r1 = lv - hi
        mid = r1.astype(BF16).astype(F32)
        lo = (r1 - mid).astype(BF16).astype(F32)
        for r in range(4 * XC):
            t = jnp.where(
                sub16 == 0, hi[r:r + 1, :],
                jnp.where(sub16 == 1, mid[r:r + 1, :],
                          jnp.where(sub16 == 2, lo[r:r + 1, :],
                                    jnp.where(sub16 == 3, 1.0, 0.0))))
            iaug[r // 4, 64:80, (r % 4) * 128:(r % 4 + 1) * 128] = t.astype(BF16)

    put_lambda()
    minus = jnp.where(sub64 < 3, -1.0, 0.0)

    def put_raw(b):
        for h in range(2):
            blk = ut[b, :, h * 128:(h + 1) * 128].astype(F32)
            rows = pl.ds(pl.multiple_of(b * 256 + h * 128, 128), 128)
            uraw[rows, :] = jnp.concatenate([blk, minus], axis=0).T.astype(BF16)

    put_raw(yl)
    pl.semaphore_wait(barrier, len(peers))

    pending = []
    gu = copies(ut.at[yl], ut.at[yl], gu_s, gu_r, lpeers)
    gi = [
        send(own_items, own_items, gi_s.at[k], gi_r.at[k], dev((x + d) % X, y, c, z))
        for k, d in enumerate(near)
    ]
    blocks = [(xc, None)]
    if C > 1:
        half = X - 1
        other = dev(x, y, 1 - c, z)
        blocks.append((x * C + 1 - c, send(
            own_items, own_items, gi_s.at[half], gi_r.at[half], other)))
        pending.append(blocks[-1][1])

    def relay(k):
        gi[k].wait_recv()
        src = (x + X - near[k]) % X
        blocks.append((src * C + c, None))
        if C > 1:
            ref = iaug.at[src * C + c, pl.ds(0, 64), :]
            q = send(ref, ref, gi_s.at[X + k], gi_r.at[X + k], other)
            pending.append(q)
            blocks.append((src * C + 1 - c, q))

    def put_users(muv):
        coef = owv + muv
        coef = jnp.where(lane < 64, coef, 1.0)
        for r in range(0, NU, 128):
            rows = slice(r, r + 128)
            sc = (uraw[rows, :].astype(F32) * coef).astype(BF16).astype(F32) * (1.0 / TAU)
            uaug[rows, :] = sc.astype(BF16)

    def logits(b, first):
        zt = jnp.dot(uaug[...], iaug[b], preferred_element_type=F32)
        zbuf[b] = zt
        m = jnp.maximum(jnp.maximum(zt[:, 0:128], zt[:, 128:256]),
                        jnp.maximum(zt[:, 256:384], zt[:, 384:512]))
        macc[...] = m if first else jnp.maximum(macc[...], m)

    def pass1_step(b, carry):
        logits(b, False)
        return carry

    def pass2_step(b, carry):
        mb = macc[...]
        parts = [jnp.exp(zbuf[b, :, k * 128:(k + 1) * 128] - mb) for k in range(4)]
        e16 = jnp.concatenate(parts, axis=1).astype(BF16)
        ebuf[b] = e16
        tacc[...] += lax.dot_general(
            e16, iaug[b], (((1,), (1,)), ((), ())), preferred_element_type=F32)
        return carry

    def lse(v):
        top = jnp.max(v, axis=0)
        return top + jnp.log(jnp.sum(jnp.exp(v - top[None]), axis=0))

    for it in range(ITERS):
        if it == 0:
            for k in range(min(2, len(near))):
                relay(k)
            for q in gu:
                q.wait_recv()
            for d in range(1, YL):
                put_raw((yl + d) % YL)
            put_users(mu)
            for k in range(XC):
                if k >= 2 and len(blocks) < XC:
                    relay(len(near) - 1)
                b, q = blocks[k]
                if q is not None:
                    q.wait_recv()
                logits(b, k == 0)
            pending += gu + gi
        else:
            logits(0, True)
            lax.fori_loop(1, XC, pass1_step, 0, unroll=True)
        for q in range(NC):
            rows = slice(q * 128, (q + 1) * 128)
            m = jnp.max(macc[rows, :], axis=1, keepdims=True)
            macc[rows, :] = jnp.broadcast_to(m, (128, 128))
        tacc[...] = jnp.zeros((NU, 128), F32)

        lax.fori_loop(0, XC, pass2_step, 0, unroll=2)

        for q in range(NC):
            rows = slice(q * 128, (q + 1) * 128)
            pt = jnp.where(lane128 == 64, macc[rows, :], tacc[rows, :]).T
            uf = ut[q // 2, :, (q % 2) * 128:(q % 2 + 1) * 128].astype(F32)
            prod = uf * pt[0:64, :]
            st[0, q:q + 1, :] = pt[64:65, :]
            st[1, q:q + 1, :] = pt[67:68, :]
            for k in range(4):
                st[2 + k, q:q + 1, :] = jnp.sum(prod[16 * k:16 * k + 16, :], axis=0, keepdims=True)

        m_loc = st[0]
        s_loc = st[1]
        yll[it, y] = m_loc + jnp.log(s_loc)
        cy_l = copies(yll.at[it, y], yll.at[it, y], yl_s.at[it], yl_r.at[it], ypeers)
        inv = 1.0 / s_loc
        for k in range(4):
            yn[it, y, k] = st[2 + k] * inv
        cy_n = copies(yn.at[it, y], yn.at[it, y], yn_s.at[it], yn_r.at[it], ypeers)
        for q in cy_l:
            q.wait_recv()
        lv = yll[it]
        ly = lse(lv)
        zll[it, z] = ly
        cz_l = copies(zll.at[it, z], zll.at[it, z], zl_s.at[it], zl_r.at[it], zpeers)
        fy = jnp.exp(lv - ly[None])
        for q in cy_n:
            q.wait_recv()
        nv = yn[it]
        for k in range(4):
            zn[it, z, k] = jnp.sum(nv[:, k] * fy, axis=0)
        cz_n = copies(zn.at[it, z], zn.at[it, z], zn_s.at[it], zn_r.at[it], zpeers)
        for q in cz_l:
            q.wait_recv()
        lv = zll[it]
        lg = lse(lv)
        w = jnp.exp(m_loc - lg)
        if it == ITERS - 1:
            macc[0:NC, :] = TAU * lg
            soft_out[...] = macc[pl.ds(yl * 2, 2), :]
        whi = w.astype(BF16).astype(F32)
        r1 = w - whi
        wmid = r1.astype(BF16).astype(F32)
        wlo = (r1 - wmid).astype(BF16).astype(F32)
        for q in range(NC):
            t = jnp.where(
                sub16 == 0, whi[q:q + 1, :],
                jnp.where(sub16 == 1, wmid[q:q + 1, :],
                          jnp.where(sub16 == 2, wlo[q:q + 1, :], 0.0)))
            wl[:, q * 128:(q + 1) * 128] = t.astype(BF16)
        for b in range(XC):
            acc = jnp.dot(wl[...], ebuf[b], preferred_element_type=F32)
            row = acc[0:1, :] + acc[1:2, :] + acc[2:3, :]
            for k in range(4):
                xload[it, xc, 4 * b + k:4 * b + k + 1, :] = row[:, k * 128:(k + 1) * 128]
        cx_l = copies(xload.at[it, xc], xload.at[it, xc], xl_s.at[it], xl_r.at[it], xpeers)
        fz = jnp.exp(lv - lg[None])
        for q in cz_n:
            q.wait_recv()
        nv = zn[it]
        xach[it, xc] = jnp.zeros((8, 128), F32)
        for k in range(4):
            t = jnp.sum(nv[:, k] * fz, axis=0)
            xach[it, xc, k:k + 1, :] = jnp.sum(t, axis=0, keepdims=True)
        cx_a = copies(xach.at[it, xc], xach.at[it, xc], xa_s.at[it], xa_r.at[it], xpeers)
        for q in cx_l:
            q.wait_recv()
        load = jnp.sum(xload[it], axis=0)
        lam[...] = jnp.maximum(
            0.0, lam[...] + DUAL_STEP * (load * (items_total / users_total) - capl[...]))
        if it < ITERS - 1:
            put_lambda()
        else:
            agbuf[yl] = lam[...]
            ca = copies(agbuf.at[yl], agbuf.at[yl], ag_s, ag_r, lpeers)
        for q in cx_a:
            q.wait_recv()
        ach = jnp.sum(jnp.sum(xach[it], axis=0), axis=1, keepdims=True) / users_total
        achv = by_tower([ach[k:k + 1, :] for k in range(4)], 0.0)
        mu = mu + TARGET_STEP * (otv - achv)
        if it < ITERS - 1:
            put_users(mu)
        pending += cy_l + cy_n + cz_l + cz_n + cx_l + cx_a

    for k in range(4):
        obj_out[k] = jnp.max(jnp.where(lane == 16 * k, mu, -3.0e38))
    for q in ca:
        q.wait_recv()
    for l in range(YL):
        for xx in range(X):
            cap_out[(xx * YL + l) * RX:(xx * YL + l + 1) * RX, :] = agbuf[l, xx * RX:(xx + 1) * RX, :]
    for q in pending + ca:
        q.wait_send()


def per_device(g, user_emb, item_emb, ow, ot, od, duals, cap):
    X, YL, C, YH, Z = g.X, g.YL, g.C, g.YH, g.Z
    Y, XC, NU = YL * YH, X * C, UD * YL
    NC = NU // 128
    rows = IB * X * YL * C // 128
    vm = pl.BlockSpec(memory_space=pltpu.VMEM)
    sm = pl.BlockSpec(memory_space=pltpu.SMEM)
    hbm = pl.BlockSpec(memory_space=pl.ANY)
    dma = pltpu.SemaphoreType.DMA
    V = pltpu.VMEM
    nl = max(YL - 1, 1)
    soft, capo, obj = pl.pallas_call(
        functools.partial(kernel, g),
        out_shape=(
            jax.ShapeDtypeStruct((UD // 128, 128), F32),
            jax.ShapeDtypeStruct((rows, 128), F32),
            jax.ShapeDtypeStruct((4,), F32),
        ),
        in_specs=[hbm, hbm, hbm, hbm, sm, sm, sm],
        out_specs=(vm, vm, sm),
        scratch_shapes=[
            V((YL, 64, UD), BF16),
            V((NU, KD), BF16),
            V((XC, KD, IB), BF16),
            V((NU, KD), BF16),
            V((XC, NU, IB), F32),
            V((XC, NU, IB), BF16),
            V((NU, 128), F32),
            V((NU, 128), F32),
            V((6, NC, 128), F32),
            V((16, NU), BF16),
            V((4 * XC, 128), F32),
            V((4 * XC, 128), F32),
            V((ITERS, Y, NC, 128), F32),
            V((ITERS, Y, 4, NC, 128), F32),
            V((ITERS, Z, NC, 128), F32),
            V((ITERS, Z, 4, NC, 128), F32),
            V((ITERS, XC, 4 * XC, 128), F32),
            V((ITERS, XC, 8, 128), F32),
            V((YL, 4 * XC, 128), F32),
            dma((2 + 2 * X,)),
            dma((2 * X,)), dma((2 * X,)), dma((nl,)), dma((nl,)),
            dma((ITERS, Y - 1)), dma((ITERS, Y - 1)), dma((ITERS, Y - 1)), dma((ITERS, Y - 1)),
            dma((ITERS, Z - 1)), dma((ITERS, Z - 1)), dma((ITERS, Z - 1)), dma((ITERS, Z - 1)),
            dma((ITERS, XC - 1)), dma((ITERS, XC - 1)), dma((ITERS, XC - 1)), dma((ITERS, XC - 1)),
            dma((nl,)), dma((nl,)),
        ],
        compiler_params=pltpu.CompilerParams(
            collective_id=0, has_side_effects=True, vmem_limit_bytes=60 * 1024 * 1024),
        name="dual_ascent",
    )(user_emb.T, item_emb, duals.reshape(rows, 128), cap.reshape(rows, 128), ow, ot, od)
    return soft.reshape(UD), capo.reshape(rows * 128), obj


def solution(mesh, g=SLICE):
    in_specs = (P("user", None), P(None, ("item", "user")), P(), P(), P(), P("item"), P("item"))
    out_specs = (P("user"), P("item"), P())
    return jax.shard_map(
        functools.partial(per_device, g), mesh=mesh, in_specs=in_specs, out_specs=out_specs,
        check_vma=False,
    )
```

time: 102 us -> 71.7 us (0.70)
  Pallas kernels: 96.1 us -> 67.6 us
  local copies, waits for them, and re-layouts: 4.72 us -> 3.22 us
    pallas_call x1, Pallas kernels: 96.1 us -> 67.6 us  [per_device(): pl.pallas_call(functools.partial(kernel, g), out_shape=(jax.ShapeDtypeStr...]
    unnamed x8 -> x7, local copies, waits for them, and re-layouts: 4.72 us -> 3.22 us
where the time goes in v2:
time: 71.7 us; the launch traced here: 71.5 us
  Pallas kernels  67.6 us (94%)
  local copies, waits for them, and re-layouts  3.22 us (4%)
    pallas_call x1, Pallas kernels, per_device(): pl.pallas_call(functools.partial(kernel, g), out_shape=(jax.ShapeDtypeStr...  67.6 us
    unnamed x7, local copies, waits for them, and re-layouts  3.22 us

profile of v2, /device:TPU:1, one launch (start us, length us, event | category | flops | bytes accessed | tf_op | source)
XLA Modules:
  0.0 71.5 jit_solution(9157483213092219788)
XLA Ops:
  0.6 67.6 %dual_ascent.1 = (f32[2,128]{1,0:T(2,128)}, f32[128,128]{1,0:T(8,128)}, f32[4]{0:T(128)}) custom-call(bf16[64,256]{1,0:T(8,128)(2,1)} %bitcast.8, bf16[64,512]{1,0:T(8,128)(2,1)} %item_hbm.1, f32[128,128]{1,0:T(8,128)} %bitcast.5, f32[128,128]{1,0:T(8,128)} %bitcast.6, f32[4]{0:T(128)} %ow_ref.1, f32[4]{0:T(128)} %ot_ref.1, f32[4]{0:T(128)} %od_ref.1), custom_call_target="tpu_custom_call" | custom-call | tf_op jit(solution)/shard_map/dual_ascent/pallas_call | solution.py:331
  68.3 0.0 copy-start
  68.3 0.7 copy-done
  68.9 0.6 copy.13
  69.5 0.0 copy-start.1
  69.5 1.5 %copy.14 = f32[16384]{0:T(1024)} copy(f32[16384]{0:T(1024)} %bitcast.7) | data formatting | bytes 131072
  71.0 0.0 copy-done.1
  71.0 0.5 copy.15
Async XLA Ops:
  68.3 0.7 copy-start
  69.5 1.5 %copy-start.1 = (f32[4]{0:T(128)S(1)}, f32[4]{0:T(128)}, u32[]{:S(2)}) copy-start(f32[4]{0:T(128)} %get-tuple-element.14) | copy-start | bytes 52

commit v3 on v2

--- a/solution.py
+++ b/solution.py
@@ -25,9 +25,10 @@
 
 def kernel(
     g,
-    user_hbm, item_hbm, duals_hbm, cap_hbm, ow_ref, ot_ref, od_ref,
-    soft_out, cap_out, obj_out,
-    ut, uraw, iaug, uaug, zbuf, ebuf, macc, tacc, st, wl, lam, capl,
+    user_hbm, item_hbm, duals_hbm, cap_hbm, ow_hbm, ot_hbm, od_hbm,
+    out,
+    ow_ref, ot_ref, od_ref,
+    ut, uraw, iaug, uaug, zbuf, ebuf, macc, sacc, tacc, st, wl, lam, capl,
     yll, yn, zll, zn, xload, xach, agbuf,
     in_s, gi_s, gi_r, gu_s, gu_r,
     yl_s, yl_r, yn_s, yn_r, zl_s, zl_r, zn_s, zn_r,
@@ -55,7 +56,6 @@
     def far_first(n):
         return sorted(range(1, n), key=lambda d: -min(d, n - d))
 
-    near = far_first(X)[::-1]
     ypeers = [dev(x, (y + d) % Y, c, z) for d in far_first(Y)]
     zpeers = [dev(x, y, c, (z + d) % Z) for d in far_first(Z)]
     xpeers = [
@@ -73,13 +73,17 @@
     local = [
         pltpu.make_async_copy(user_hbm, ut.at[yl], in_s.at[0]),
         pltpu.make_async_copy(item_hbm, own_items, in_s.at[1]),
+        pltpu.make_async_copy(ow_hbm, ow_ref, in_s.at[2]),
+        pltpu.make_async_copy(ot_hbm, ot_ref, in_s.at[3]),
+        pltpu.make_async_copy(od_hbm, od_ref, in_s.at[4]),
     ]
     RX = 4 * C
+    rows_out = RX * X * YL
     for xx in range(X):
         rows = pl.ds(pl.multiple_of((xx * YL + yl) * RX, RX), RX)
         mine = pl.ds(xx * RX, RX)
-        local.append(pltpu.make_async_copy(duals_hbm.at[rows], lam.at[mine], in_s.at[2 + 2 * xx]))
-        local.append(pltpu.make_async_copy(cap_hbm.at[rows], capl.at[mine], in_s.at[3 + 2 * xx]))
+        local.append(pltpu.make_async_copy(duals_hbm.at[rows], lam.at[mine], in_s.at[5 + 2 * xx]))
+        local.append(pltpu.make_async_copy(cap_hbm.at[rows], capl.at[mine], in_s.at[6 + 2 * xx]))
     for q in local:
         q.start()
     for b in range(XC):
@@ -141,27 +145,32 @@
 
     pending = []
     gu = copies(ut.at[yl], ut.at[yl], gu_s, gu_r, lpeers)
-    gi = [
-        send(own_items, own_items, gi_s.at[k], gi_r.at[k], dev((x + d) % X, y, c, z))
-        for k, d in enumerate(near)
-    ]
-    blocks = [(xc, None)]
-    if C > 1:
-        half = X - 1
-        other = dev(x, y, 1 - c, z)
-        blocks.append((x * C + 1 - c, send(
-            own_items, own_items, gi_s.at[half], gi_r.at[half], other)))
-        pending.append(blocks[-1][1])
-
-    def relay(k):
-        gi[k].wait_recv()
-        src = (x + X - near[k]) % X
-        blocks.append((src * C + c, None))
-        if C > 1:
-            ref = iaug.at[src * C + c, pl.ds(0, 64), :]
-            q = send(ref, ref, gi_s.at[X + k], gi_r.at[X + k], other)
-            pending.append(q)
-            blocks.append((src * C + 1 - c, q))
+    fwd, bwd = (x + 1) % X, (x + X - 1) % X
+    opp = (x + 2) % X
+    nxt, prv, other = dev(fwd, y, c, z), dev(bwd, y, c, z), dev(x, y, 1 - c, z)
+
+    def items(x_, part=None):
+        r = pl.ds(0, 64) if part is None else pl.ds(32 * part, 32)
+        return iaug.at[x_ * C + c, r, :]
+
+    def gsend(x_, part, k, target):
+        q = send(items(x_, part), items(x_, part), gi_s.at[k], gi_r.at[k], target)
+        pending.append(q)
+        return q
+
+    f0 = gsend(x, 0, 0, nxt)
+    b1 = gsend(x, 1, 1, prv)
+    own = gsend(x, None, 2, other)
+    f1 = gsend(x, 1, 3, nxt)
+    b0 = gsend(x, 0, 4, prv)
+    f0.wait_recv()
+    fo = gsend(bwd, 0, 5, nxt)
+    b1.wait_recv()
+    bo = gsend(fwd, 1, 6, prv)
+    f1.wait_recv()
+    cb = gsend(bwd, None, 7, other)
+    b0.wait_recv()
+    cf = gsend(fwd, None, 8, other)
 
     def put_users(muv):
         coef = owv + muv
@@ -182,14 +191,30 @@
         logits(b, False)
         return carry
 
-    def pass2_step(b, carry):
+    def towers(e16, b):
+        tacc[...] += lax.dot_general(
+            e16, iaug[b], (((1,), (1,)), ((), ())), preferred_element_type=F32)
+
+    def pass2_step(last, b, carry):
         mb = macc[...]
         parts = [jnp.exp(zbuf[b, :, k * 128:(k + 1) * 128] - mb) for k in range(4)]
         e16 = jnp.concatenate(parts, axis=1).astype(BF16)
         ebuf[b] = e16
-        tacc[...] += lax.dot_general(
-            e16, iaug[b], (((1,), (1,)), ((), ())), preferred_element_type=F32)
+        if last:
+            sacc[...] += (parts[0] + parts[1]) + (parts[2] + parts[3])
+        else:
+            towers(e16, b)
         return carry
+
+    def towers_step(b, carry):
+        towers(ebuf[b], b)
+        return carry
+
+    def put_numerators(q, pt):
+        uf = ut[q // 2, :, (q % 2) * 128:(q % 2 + 1) * 128].astype(F32)
+        prod = uf * pt[0:64, :]
+        for k in range(4):
+            st[2 + k, q:q + 1, :] = jnp.sum(prod[16 * k:16 * k + 16, :], axis=0, keepdims=True)
 
     def lse(v):
         top = jnp.max(v, axis=0)
@@ -197,21 +222,27 @@
 
     for it in range(ITERS):
         if it == 0:
-            for k in range(min(2, len(near))):
-                relay(k)
             for q in gu:
                 q.wait_recv()
             for d in range(1, YL):
                 put_raw((yl + d) % YL)
             put_users(mu)
-            for k in range(XC):
-                if k >= 2 and len(blocks) < XC:
-                    relay(len(near) - 1)
-                b, q = blocks[k]
-                if q is not None:
-                    q.wait_recv()
-                logits(b, k == 0)
-            pending += gu + gi
+            logits(x * C + c, True)
+            own.wait_recv()
+            logits(x * C + 1 - c, False)
+            logits(bwd * C + c, False)
+            logits(fwd * C + c, False)
+            fo.wait_recv()
+            bo.wait_recv()
+            co = gsend(opp, None, 9, other)
+            cb.wait_recv()
+            logits(bwd * C + 1 - c, False)
+            cf.wait_recv()
+            logits(fwd * C + 1 - c, False)
+            logits(opp * C + c, False)
+            co.wait_recv()
+            logits(opp * C + 1 - c, False)
+            pending += gu
         else:
             logits(0, True)
             lax.fori_loop(1, XC, pass1_step, 0, unroll=True)
@@ -219,25 +250,35 @@
             rows = slice(q * 128, (q + 1) * 128)
             m = jnp.max(macc[rows, :], axis=1, keepdims=True)
             macc[rows, :] = jnp.broadcast_to(m, (128, 128))
+        last = it == ITERS - 1
         tacc[...] = jnp.zeros((NU, 128), F32)
-
-        lax.fori_loop(0, XC, pass2_step, 0, unroll=2)
+        if last:
+            sacc[...] = jnp.zeros((NU, 128), F32)
+
+        lax.fori_loop(0, XC, functools.partial(pass2_step, last), 0, unroll=4)
 
         for q in range(NC):
             rows = slice(q * 128, (q + 1) * 128)
-            pt = jnp.where(lane128 == 64, macc[rows, :], tacc[rows, :]).T
-            uf = ut[q // 2, :, (q % 2) * 128:(q % 2 + 1) * 128].astype(F32)
-            prod = uf * pt[0:64, :]
+            if last:
+                sv = sacc[rows, :]
+                sv = sv + pltpu.roll(sv, 64, 1)
+                pt = jnp.where(lane128 < 64, sv, macc[rows, :]).T
+                st[1, q:q + 1, :] = jnp.sum(pt[0:64, :], axis=0, keepdims=True)
+            else:
+                pt = jnp.where(lane128 == 64, macc[rows, :], tacc[rows, :]).T
+                st[1, q:q + 1, :] = pt[67:68, :]
+                put_numerators(q, pt)
             st[0, q:q + 1, :] = pt[64:65, :]
-            st[1, q:q + 1, :] = pt[67:68, :]
-            for k in range(4):
-                st[2 + k, q:q + 1, :] = jnp.sum(prod[16 * k:16 * k + 16, :], axis=0, keepdims=True)
 
         m_loc = st[0]
         s_loc = st[1]
         yll[it, y] = m_loc + jnp.log(s_loc)
         cy_l = copies(yll.at[it, y], yll.at[it, y], yl_s.at[it], yl_r.at[it], ypeers)
         inv = 1.0 / s_loc
+        if last:
+            lax.fori_loop(0, XC, towers_step, 0, unroll=4)
+            for q in range(NC):
+                put_numerators(q, tacc[q * 128:(q + 1) * 128, :].T)
         for k in range(4):
             yn[it, y, k] = st[2 + k] * inv
         cy_n = copies(yn.at[it, y], yn.at[it, y], yn_s.at[it], yn_r.at[it], ypeers)
@@ -259,9 +300,9 @@
         lv = zll[it]
         lg = lse(lv)
         w = jnp.exp(m_loc - lg)
-        if it == ITERS - 1:
+        if last:
             macc[0:NC, :] = TAU * lg
-            soft_out[...] = macc[pl.ds(yl * 2, 2), :]
+            out[rows_out:rows_out + 2, :] = macc[pl.ds(yl * 2, 2), :]
         whi = w.astype(BF16).astype(F32)
         r1 = w - whi
         wmid = r1.astype(BF16).astype(F32)
@@ -272,12 +313,15 @@
                 jnp.where(sub16 == 1, wmid[q:q + 1, :],
                           jnp.where(sub16 == 2, wlo[q:q + 1, :], 0.0)))
             wl[:, q * 128:(q + 1) * 128] = t.astype(BF16)
-        for b in range(XC):
-            acc = jnp.dot(wl[...], ebuf[b], preferred_element_type=F32)
-            row = acc[0:1, :] + acc[1:2, :] + acc[2:3, :]
-            for k in range(4):
-                xload[it, xc, 4 * b + k:4 * b + k + 1, :] = row[:, k * 128:(k + 1) * 128]
-        cx_l = copies(xload.at[it, xc], xload.at[it, xc], xl_s.at[it], xl_r.at[it], xpeers)
+        cx_l = []
+        for h in range(2):
+            for b in range(h * XC // 2, (h + 1) * XC // 2):
+                acc = jnp.dot(wl[...], ebuf[b], preferred_element_type=F32)
+                row = acc[0:1, :] + acc[1:2, :] + acc[2:3, :]
+                for k in range(4):
+                    xload[it, xc, 4 * b + k:4 * b + k + 1, :] = row[:, k * 128:(k + 1) * 128]
+            part = xload.at[it, xc, pl.ds(2 * XC * h, 2 * XC), :]
+            cx_l += copies(part, part, xl_s.at[it, h], xl_r.at[it, h], xpeers)
         fz = jnp.exp(lv - lg[None])
         for q in cz_n:
             q.wait_recv()
@@ -292,7 +336,7 @@
         load = jnp.sum(xload[it], axis=0)
         lam[...] = jnp.maximum(
             0.0, lam[...] + DUAL_STEP * (load * (items_total / users_total) - capl[...]))
-        if it < ITERS - 1:
+        if not last:
             put_lambda()
         else:
             agbuf[yl] = lam[...]
@@ -302,19 +346,27 @@
         ach = jnp.sum(jnp.sum(xach[it], axis=0), axis=1, keepdims=True) / users_total
         achv = by_tower([ach[k:k + 1, :] for k in range(4)], 0.0)
         mu = mu + TARGET_STEP * (otv - achv)
-        if it < ITERS - 1:
+        if not last:
             put_users(mu)
         pending += cy_l + cy_n + cz_l + cz_n + cx_l + cx_a
 
-    for k in range(4):
-        obj_out[k] = jnp.max(jnp.where(lane == 16 * k, mu, -3.0e38))
+    out[rows_out + 2:rows_out + 3, :] = mu
     for q in ca:
         q.wait_recv()
     for l in range(YL):
         for xx in range(X):
-            cap_out[(xx * YL + l) * RX:(xx * YL + l + 1) * RX, :] = agbuf[l, xx * RX:(xx + 1) * RX, :]
+            out[(xx * YL + l) * RX:(xx * YL + l + 1) * RX, :] = agbuf[l, xx * RX:(xx + 1) * RX, :]
     for q in pending + ca:
         q.wait_send()
+
+
+def split_out(rows, packed, soft_out, cap_out, obj_out):
+    cap_out[...] = packed[0:rows, :]
+    soft_out[...] = packed[rows:rows + 2, :]
+    lane = lax.broadcasted_iota(jnp.int32, (1, 128), 1)
+    mu = packed[rows + 2:rows + 3, :]
+    for k in range(4):
+        obj_out[k] = jnp.max(jnp.where(lane == 16 * k, mu, -3.0e38))
 
 
 def per_device(g, user_emb, item_emb, ow, ot, od, duals, cap):
@@ -328,22 +380,20 @@
     dma = pltpu.SemaphoreType.DMA
     V = pltpu.VMEM
     nl = max(YL - 1, 1)
-    soft, capo, obj = pl.pallas_call(
+    packed = pl.pallas_call(
         functools.partial(kernel, g),
-        out_shape=(
-            jax.ShapeDtypeStruct((UD // 128, 128), F32),
-            jax.ShapeDtypeStruct((rows, 128), F32),
-            jax.ShapeDtypeStruct((4,), F32),
-        ),
-        in_specs=[hbm, hbm, hbm, hbm, sm, sm, sm],
-        out_specs=(vm, vm, sm),
+        out_shape=jax.ShapeDtypeStruct((rows + 8, 128), F32),
+        in_specs=[hbm] * 7,
+        out_specs=vm,
         scratch_shapes=[
+            pltpu.SMEM((4,), F32), pltpu.SMEM((4,), F32), pltpu.SMEM((4,), F32),
             V((YL, 64, UD), BF16),
             V((NU, KD), BF16),
             V((XC, KD, IB), BF16),
             V((NU, KD), BF16),
             V((XC, NU, IB), F32),
             V((XC, NU, IB), BF16),
+            V((NU, 128), F32),
             V((NU, 128), F32),
             V((NU, 128), F32),
             V((6, NC, 128), F32),
@@ -357,17 +407,28 @@
             V((ITERS, XC, 4 * XC, 128), F32),
             V((ITERS, XC, 8, 128), F32),
             V((YL, 4 * XC, 128), F32),
-            dma((2 + 2 * X,)),
-            dma((2 * X,)), dma((2 * X,)), dma((nl,)), dma((nl,)),
+            dma((5 + 2 * X,)),
+            dma((10,)), dma((10,)), dma((nl,)), dma((nl,)),
             dma((ITERS, Y - 1)), dma((ITERS, Y - 1)), dma((ITERS, Y - 1)), dma((ITERS, Y - 1)),
             dma((ITERS, Z - 1)), dma((ITERS, Z - 1)), dma((ITERS, Z - 1)), dma((ITERS, Z - 1)),
-            dma((ITERS, XC - 1)), dma((ITERS, XC - 1)), dma((ITERS, XC - 1)), dma((ITERS, XC - 1)),
+            dma((ITERS, 2, XC - 1)), dma((ITERS, 2, XC - 1)), dma((ITERS, XC - 1)), dma((ITERS, XC - 1)),
             dma((nl,)), dma((nl,)),
         ],
         compiler_params=pltpu.CompilerParams(
             collective_id=0, has_side_effects=True, vmem_limit_bytes=60 * 1024 * 1024),
         name="dual_ascent",
     )(user_emb.T, item_emb, duals.reshape(rows, 128), cap.reshape(rows, 128), ow, ot, od)
+    soft, capo, obj = pl.pallas_call(
+        functools.partial(split_out, rows),
+        out_shape=(
+            jax.ShapeDtypeStruct((UD // 128, 128), F32),
+            jax.ShapeDtypeStruct((rows, 128), F32),
+            jax.ShapeDtypeStruct((4,), F32),
+        ),
+        in_specs=[vm],
+        out_specs=(vm, vm, sm),
+        name="split_out",
+    )(packed)
     return soft.reshape(UD), capo.reshape(rows * 128), obj
 
 

time: 71.7 us -> 72.3 us (level)
  Pallas kernels: 67.6 us -> 71.3 us
  local copies, waits for them, and re-layouts: 3.22 us -> 0 us
    pallas_call x1 -> x2, Pallas kernels: 67.6 us -> 71.3 us  [the longest x1 69.8 us: per_device(): pl.pallas_call(functools.partial(kernel, g), out_shape=jax.ShapeDtypeStru...]
    unnamed x7 -> x0, local copies, waits for them, and re-layouts: 3.22 us -> none
where the time goes in v3:
time: 72.3 us; the launch traced here: 72.1 us
  Pallas kernels  71.3 us (99%)
  between operations  0.8 us (1%)
    pallas_call x1, Pallas kernels, per_device(): pl.pallas_call(functools.partial(kernel, g), out_shape=jax.ShapeDtypeStru...  69.8 us
    pallas_call x1, Pallas kernels, per_device(): pl.pallas_call(functools.partial(split_out, rows), out_shape=(jax.ShapeDt...  1.53 us

profile of v3, /device:TPU:1, one launch (start us, length us, event | category | flops | bytes accessed | tf_op | source)
XLA Modules:
  0.0 72.1 jit_solution(9217853218483576828)
XLA Ops:
  0.6 69.8 %dual_ascent.1.packed = f32[136,128]{1,0:T(8,128)} custom-call(bf16[64,256]{1,0:T(8,128)(2,1)} %bitcast.7, bf16[64,512]{1,0:T(8,128)(2,1)} %item_hbm.1, f32[128,128]{1,0:T(8,128)} %bitcast.5, f32[128,128]{1,0:T(8,128)} %bitcast.6, f32[4]{0:T(128)} %ow_hbm.1, f32[4]{0:T(128)} %ot_hbm.1, f32[4]{0:T(128)} %od_hbm.1), custom_call_target="tpu_custom_call" | custom-call | tf_op jit(solution)/shard_map/dual_ascent/pallas_call | solution.py:383
  70.4 1.5 %split_out.1 = (f32[2,128]{1,0:T(2,128)}, f32[128,128]{1,0:T(8,128)}, f32[4]{0:T(128)}) custom-call(f32[136,128]{1,0:T(8,128)} %dual_ascent.1.packed), custom_call_target="tpu_custom_call" | custom-call | tf_op jit(solution)/shard_map/split_out/pallas_call | solution.py:421

commit v4 on v3

--- a/solution.py
+++ b/solution.py
@@ -28,7 +28,7 @@
     user_hbm, item_hbm, duals_hbm, cap_hbm, ow_hbm, ot_hbm, od_hbm,
     out,
     ow_ref, ot_ref, od_ref,
-    ut, uraw, iaug, uaug, zbuf, ebuf, macc, sacc, tacc, st, wl, lam, capl,
+    ut, uraw, iaug, uaug, zbuf, ebuf, macc, tacc, st, wl, lam, capl,
     yll, yn, zll, zn, xload, xach, agbuf,
     in_s, gi_s, gi_r, gu_s, gu_r,
     yl_s, yl_r, yn_s, yn_r, zl_s, zl_r, zn_s, zn_r,
@@ -158,16 +158,12 @@
         pending.append(q)
         return q
 
-    f0 = gsend(x, 0, 0, nxt)
-    b1 = gsend(x, 1, 1, prv)
+    far = dev(opp, y, c, z)
+    f0 = gsend(x, None, 0, nxt)
+    b0 = gsend(x, None, 1, prv)
+    fo = gsend(x, None, 3, far)
     own = gsend(x, None, 2, other)
-    f1 = gsend(x, 1, 3, nxt)
-    b0 = gsend(x, 0, 4, prv)
     f0.wait_recv()
-    fo = gsend(bwd, 0, 5, nxt)
-    b1.wait_recv()
-    bo = gsend(fwd, 1, 6, prv)
-    f1.wait_recv()
     cb = gsend(bwd, None, 7, other)
     b0.wait_recv()
     cf = gsend(fwd, None, 8, other)
@@ -191,23 +187,13 @@
         logits(b, False)
         return carry
 
-    def towers(e16, b):
-        tacc[...] += lax.dot_general(
-            e16, iaug[b], (((1,), (1,)), ((), ())), preferred_element_type=F32)
-
-    def pass2_step(last, b, carry):
+    def pass2_step(b, carry):
         mb = macc[...]
         parts = [jnp.exp(zbuf[b, :, k * 128:(k + 1) * 128] - mb) for k in range(4)]
         e16 = jnp.concatenate(parts, axis=1).astype(BF16)
         ebuf[b] = e16
-        if last:
-            sacc[...] += (parts[0] + parts[1]) + (parts[2] + parts[3])
-        else:
-            towers(e16, b)
-        return carry
-
-    def towers_step(b, carry):
-        towers(ebuf[b], b)
+        tacc[...] += lax.dot_general(
+            e16, iaug[b], (((1,), (1,)), ((), ())), preferred_element_type=F32)
         return carry
 
     def put_numerators(q, pt):
@@ -233,7 +219,6 @@
             logits(bwd * C + c, False)
             logits(fwd * C + c, False)
             fo.wait_recv()
-            bo.wait_recv()
             co = gsend(opp, None, 9, other)
             cb.wait_recv()
             logits(bwd * C + 1 - c, False)
@@ -252,22 +237,14 @@
             macc[rows, :] = jnp.broadcast_to(m, (128, 128))
         last = it == ITERS - 1
         tacc[...] = jnp.zeros((NU, 128), F32)
-        if last:
-            sacc[...] = jnp.zeros((NU, 128), F32)
-
-        lax.fori_loop(0, XC, functools.partial(pass2_step, last), 0, unroll=4)
+
+        lax.fori_loop(0, XC, pass2_step, 0, unroll=4)
 
         for q in range(NC):
             rows = slice(q * 128, (q + 1) * 128)
-            if last:
-                sv = sacc[rows, :]
-                sv = sv + pltpu.roll(sv, 64, 1)
-                pt = jnp.where(lane128 < 64, sv, macc[rows, :]).T
-                st[1, q:q + 1, :] = jnp.sum(pt[0:64, :], axis=0, keepdims=True)
-            else:
-                pt = jnp.where(lane128 == 64, macc[rows, :], tacc[rows, :]).T
-                st[1, q:q + 1, :] = pt[67:68, :]
-                put_numerators(q, pt)
+            pt = jnp.where(lane128 == 64, macc[rows, :], tacc[rows, :]).T
+            st[1, q:q + 1, :] = pt[67:68, :]
+            put_numerators(q, pt)
             st[0, q:q + 1, :] = pt[64:65, :]
 
         m_loc = st[0]
@@ -275,10 +252,6 @@
         yll[it, y] = m_loc + jnp.log(s_loc)
         cy_l = copies(yll.at[it, y], yll.at[it, y], yl_s.at[it], yl_r.at[it], ypeers)
         inv = 1.0 / s_loc
-        if last:
-            lax.fori_loop(0, XC, towers_step, 0, unroll=4)
-            for q in range(NC):
-                put_numerators(q, tacc[q * 128:(q + 1) * 128, :].T)
         for k in range(4):
             yn[it, y, k] = st[2 + k] * inv
         cy_n = copies(yn.at[it, y], yn.at[it, y], yn_s.at[it], yn_r.at[it], ypeers)
@@ -313,16 +286,25 @@
                 jnp.where(sub16 == 1, wmid[q:q + 1, :],
                           jnp.where(sub16 == 2, wlo[q:q + 1, :], 0.0)))
             wl[:, q * 128:(q + 1) * 128] = t.astype(BF16)
-        cx_l = []
-        for h in range(2):
-            for b in range(h * XC // 2, (h + 1) * XC // 2):
-                acc = jnp.dot(wl[...], ebuf[b], preferred_element_type=F32)
-                row = acc[0:1, :] + acc[1:2, :] + acc[2:3, :]
-                for k in range(4):
-                    xload[it, xc, 4 * b + k:4 * b + k + 1, :] = row[:, k * 128:(k + 1) * 128]
-            part = xload.at[it, xc, pl.ds(2 * XC * h, 2 * XC), :]
-            cx_l += copies(part, part, xl_s.at[it, h], xl_r.at[it, h], xpeers)
+        for b in range(XC):
+            acc = jnp.dot(wl[...], ebuf[b], preferred_element_type=F32)
+            row = acc[0:1, :] + acc[1:2, :] + acc[2:3, :]
+            for k in range(4):
+                xload[it, xc, 4 * b + k:4 * b + k + 1, :] = row[:, k * 128:(k + 1) * 128]
+        cx_l = copies(xload.at[it, xc], xload.at[it, xc], xl_s.at[it], xl_r.at[it], xpeers)
         fz = jnp.exp(lv - lg[None])
+
+        def loads_in():
+            for q in cx_l:
+                q.wait_recv()
+            load = jnp.sum(xload[it], axis=0)
+            lam[...] = jnp.maximum(
+                0.0, lam[...] + DUAL_STEP * (load * (items_total / users_total) - capl[...]))
+
+        if last:
+            loads_in()
+            agbuf[yl] = lam[...]
+            ca = copies(agbuf.at[yl], agbuf.at[yl], ag_s, ag_r, lpeers)
         for q in cz_n:
             q.wait_recv()
         nv = zn[it]
@@ -331,16 +313,9 @@
             t = jnp.sum(nv[:, k] * fz, axis=0)
             xach[it, xc, k:k + 1, :] = jnp.sum(t, axis=0, keepdims=True)
         cx_a = copies(xach.at[it, xc], xach.at[it, xc], xa_s.at[it], xa_r.at[it], xpeers)
-        for q in cx_l:
-            q.wait_recv()
-        load = jnp.sum(xload[it], axis=0)
-        lam[...] = jnp.maximum(
-            0.0, lam[...] + DUAL_STEP * (load * (items_total / users_total) - capl[...]))
         if not last:
+            loads_in()
             put_lambda()
-        else:
-            agbuf[yl] = lam[...]
-            ca = copies(agbuf.at[yl], agbuf.at[yl], ag_s, ag_r, lpeers)
         for q in cx_a:
             q.wait_recv()
         ach = jnp.sum(jnp.sum(xach[it], axis=0), axis=1, keepdims=True) / users_total
@@ -395,7 +370,6 @@
             V((XC, NU, IB), BF16),
             V((NU, 128), F32),
             V((NU, 128), F32),
-            V((NU, 128), F32),
             V((6, NC, 128), F32),
             V((16, NU), BF16),
             V((4 * XC, 128), F32),
@@ -411,7 +385,7 @@
             dma((10,)), dma((10,)), dma((nl,)), dma((nl,)),
             dma((ITERS, Y - 1)), dma((ITERS, Y - 1)), dma((ITERS, Y - 1)), dma((ITERS, Y - 1)),
             dma((ITERS, Z - 1)), dma((ITERS, Z - 1)), dma((ITERS, Z - 1)), dma((ITERS, Z - 1)),
-            dma((ITERS, 2, XC - 1)), dma((ITERS, 2, XC - 1)), dma((ITERS, XC - 1)), dma((ITERS, XC - 1)),
+            dma((ITERS, XC - 1)), dma((ITERS, XC - 1)), dma((ITERS, XC - 1)), dma((ITERS, XC - 1)),
             dma((nl,)), dma((nl,)),
         ],
         compiler_params=pltpu.CompilerParams(

time: 72.3 us -> 69.4 us (0.960)
  Pallas kernels: 71.3 us -> 68.6 us
    pallas_call x1, Pallas kernels: 69.8 us -> 67.1 us  [per_device(): pl.pallas_call(functools.partial(kernel, g), out_shape=jax.ShapeDtypeStru...]
where the time goes in v4:
time: 69.4 us; the launch traced here: 69.2 us
  Pallas kernels  68.6 us (99%)
    pallas_call x1, Pallas kernels, per_device(): pl.pallas_call(functools.partial(kernel, g), out_shape=jax.ShapeDtypeStru...  67.1 us
    pallas_call x1, Pallas kernels, per_device(): pl.pallas_call(functools.partial(split_out, rows), out_shape=(jax.ShapeDt...  1.53 us

profile of v4, /device:TPU:1, one launch (start us, length us, event | category | flops | bytes accessed | tf_op | source)
XLA Modules:
  0.0 69.2 jit_solution(10716104466315615956)
XLA Ops:
  0.6 67.1 %dual_ascent.1.packed = f32[136,128]{1,0:T(8,128)} custom-call(bf16[64,256]{1,0:T(8,128)(2,1)} %bitcast.7, bf16[64,512]{1,0:T(8,128)(2,1)} %item_hbm.1, f32[128,128]{1,0:T(8,128)} %bitcast.5, f32[128,128]{1,0:T(8,128)} %bitcast.6, f32[4]{0:T(128)} %ow_hbm.1, f32[4]{0:T(128)} %ot_hbm.1, f32[4]{0:T(128)} %od_hbm.1), custom_call_target="tpu_custom_call" | custom-call | tf_op jit(solution)/shard_map/dual_ascent/pallas_call | solution.py:358
  67.7 1.5 %split_out.1 = (f32[2,128]{1,0:T(2,128)}, f32[128,128]{1,0:T(8,128)}, f32[4]{0:T(128)}) custom-call(f32[136,128]{1,0:T(8,128)} %dual_ascent.1.packed), custom_call_target="tpu_custom_call" | custom-call | tf_op jit(solution)/shard_map/split_out/pallas_call | solution.py:395

commit v5 on v4

--- a/solution.py
+++ b/solution.py
@@ -88,7 +88,7 @@
         q.start()
     for b in range(XC):
         iaug[b, 64:128, :] = jnp.zeros((64, IB), BF16)
-    for q in local:
+    for q in local[:2]:
         q.wait()
 
     def send(src, dst, ss, rs, target):
@@ -101,6 +101,29 @@
     def copies(src, dst, ss, rs, targets):
         return [send(src, dst, ss.at[k], rs.at[k], t) for k, t in enumerate(targets)]
 
+    pl.semaphore_wait(barrier, len(peers))
+
+    pending = []
+    gu = copies(ut.at[yl], ut.at[yl], gu_s, gu_r, lpeers)
+    fwd, bwd = (x + 1) % X, (x + X - 1) % X
+    opp = (x + 2) % X
+    nxt, prv, other = dev(fwd, y, c, z), dev(bwd, y, c, z), dev(x, y, 1 - c, z)
+
+    def items(x_, part=None):
+        r = pl.ds(0, 64) if part is None else pl.ds(32 * part, 32)
+        return iaug.at[x_ * C + c, r, :]
+
+    def gsend(x_, part, k, target):
+        q = send(items(x_, part), items(x_, part), gi_s.at[k], gi_r.at[k], target)
+        pending.append(q)
+        return q
+
+    far = dev(opp, y, c, z)
+    fo = gsend(x, None, 3, far)
+    f0 = gsend(x, None, 0, nxt)
+    b0 = gsend(x, None, 1, prv)
+    own = gsend(x, None, 2, other)
+
     lane = lax.broadcasted_iota(jnp.int32, (1, 128), 1)
     tower = lane // 16
     lane128 = lax.broadcasted_iota(jnp.int32, (128, 128), 1)
@@ -113,6 +136,8 @@
             out = jnp.where(tower == k, vals[k], out)
         return out
 
+    for q in local[2:]:
+        q.wait()
     owv = by_tower([ow_ref[k] for k in range(4)], 1.0)
     otv = by_tower([ot_ref[k] for k in range(4)], 0.0)
     mu = by_tower([od_ref[k] for k in range(4)], 0.0)
@@ -141,30 +166,7 @@
             uraw[rows, :] = jnp.concatenate([blk, minus], axis=0).T.astype(BF16)
 
     put_raw(yl)
-    pl.semaphore_wait(barrier, len(peers))
-
-    pending = []
-    gu = copies(ut.at[yl], ut.at[yl], gu_s, gu_r, lpeers)
-    fwd, bwd = (x + 1) % X, (x + X - 1) % X
-    opp = (x + 2) % X
-    nxt, prv, other = dev(fwd, y, c, z), dev(bwd, y, c, z), dev(x, y, 1 - c, z)
-
-    def items(x_, part=None):
-        r = pl.ds(0, 64) if part is None else pl.ds(32 * part, 32)
-        return iaug.at[x_ * C + c, r, :]
-
-    def gsend(x_, part, k, target):
-        q = send(items(x_, part), items(x_, part), gi_s.at[k], gi_r.at[k], target)
-        pending.append(q)
-        return q
-
-    far = dev(opp, y, c, z)
-    f0 = gsend(x, None, 0, nxt)
-    b0 = gsend(x, None, 1, prv)
-    fo = gsend(x, None, 3, far)
-    own = gsend(x, None, 2, other)
-    f0.wait_recv()
-    cb = gsend(bwd, None, 7, other)
+
     b0.wait_recv()
     cf = gsend(fwd, None, 8, other)
 
@@ -214,19 +216,21 @@
                 put_raw((yl + d) % YL)
             put_users(mu)
             logits(x * C + c, True)
+            fo.wait_recv()
+            co = gsend(opp, None, 9, other)
             own.wait_recv()
             logits(x * C + 1 - c, False)
-            logits(bwd * C + c, False)
+            f0.wait_recv()
+            cb = gsend(bwd, None, 7, other)
             logits(fwd * C + c, False)
-            fo.wait_recv()
-            co = gsend(opp, None, 9, other)
-            cb.wait_recv()
-            logits(bwd * C + 1 - c, False)
             cf.wait_recv()
             logits(fwd * C + 1 - c, False)
             logits(opp * C + c, False)
+            logits(bwd * C + c, False)
             co.wait_recv()
             logits(opp * C + 1 - c, False)
+            cb.wait_recv()
+            logits(bwd * C + 1 - c, False)
             pending += gu
         else:
             logits(0, True)

time: 69.4 us -> 69.1 us (level)
  no operation moved by 1% of the time
where the time goes in v5:
time: 69.1 us; the launch traced here: 68.9 us
  Pallas kernels  68.3 us (99%)
    pallas_call x1, Pallas kernels, per_device(): pl.pallas_call(functools.partial(kernel, g), out_shape=jax.ShapeDtypeStru...  66.7 us
    pallas_call x1, Pallas kernels, per_device(): pl.pallas_call(functools.partial(split_out, rows), out_shape=(jax.ShapeDt...  1.53 us

profile of v5, /device:TPU:1, one launch (start us, length us, event | category | flops | bytes accessed | tf_op | source)
XLA Modules:
  0.0 68.9 jit_solution(5386772946524386740)
XLA Ops:
  0.6 66.7 %dual_ascent.1.packed = f32[136,128]{1,0:T(8,128)} custom-call(bf16[64,256]{1,0:T(8,128)(2,1)} %bitcast.7, bf16[64,512]{1,0:T(8,128)(2,1)} %item_hbm.1, f32[128,128]{1,0:T(8,128)} %bitcast.5, f32[128,128]{1,0:T(8,128)} %bitcast.6, f32[4]{0:T(128)} %ow_hbm.1, f32[4]{0:T(128)} %ot_hbm.1, f32[4]{0:T(128)} %od_hbm.1), custom_call_target="tpu_custom_call" | custom-call | tf_op jit(solution)/shard_map/dual_ascent/pallas_call | solution.py:362
  67.4 1.5 %split_out.1 = (f32[2,128]{1,0:T(2,128)}, f32[128,128]{1,0:T(8,128)}, f32[4]{0:T(128)}) custom-call(f32[136,128]{1,0:T(8,128)} %dual_ascent.1.packed), custom_call_target="tpu_custom_call" | custom-call | tf_op jit(solution)/shard_map/split_out/pallas_call | solution.py:399

commit v6 on v5

--- a/solution.py
+++ b/solution.py
@@ -28,7 +28,7 @@
     user_hbm, item_hbm, duals_hbm, cap_hbm, ow_hbm, ot_hbm, od_hbm,
     out,
     ow_ref, ot_ref, od_ref,
-    ut, uraw, iaug, uaug, zbuf, ebuf, macc, tacc, st, wl, lam, capl,
+    ut, uraw, iaug, uaug, zbuf, ebuf, macc, tacc, ptn, st, wl, lam, capl,
     yll, yn, zll, zn, xload, xach, agbuf,
     in_s, gi_s, gi_r, gu_s, gu_r,
     yl_s, yl_r, yn_s, yn_r, zl_s, zl_r, zn_s, zn_r,
@@ -200,7 +200,7 @@
 
     def put_numerators(q, pt):
         uf = ut[q // 2, :, (q % 2) * 128:(q % 2 + 1) * 128].astype(F32)
-        prod = uf * pt[0:64, :]
+        prod = uf * pt
         for k in range(4):
             st[2 + k, q:q + 1, :] = jnp.sum(prod[16 * k:16 * k + 16, :], axis=0, keepdims=True)
 
@@ -248,13 +248,15 @@
             rows = slice(q * 128, (q + 1) * 128)
             pt = jnp.where(lane128 == 64, macc[rows, :], tacc[rows, :]).T
             st[1, q:q + 1, :] = pt[67:68, :]
-            put_numerators(q, pt)
+            ptn[q] = pt[0:64, :]
             st[0, q:q + 1, :] = pt[64:65, :]
 
         m_loc = st[0]
         s_loc = st[1]
         yll[it, y] = m_loc + jnp.log(s_loc)
         cy_l = copies(yll.at[it, y], yll.at[it, y], yl_s.at[it], yl_r.at[it], ypeers)
+        for q in range(NC):
+            put_numerators(q, ptn[q])
         inv = 1.0 / s_loc
         for k in range(4):
             yn[it, y, k] = st[2 + k] * inv
@@ -374,6 +376,7 @@
             V((XC, NU, IB), BF16),
             V((NU, 128), F32),
             V((NU, 128), F32),
+            V((NC, 64, 128), F32),
             V((6, NC, 128), F32),
             V((16, NU), BF16),
             V((4 * XC, 128), F32),

time: 69.1 us -> 69.1 us (level)
  no operation moved by 1% of the time
where the time goes in v6:
time: 69.1 us; the launch traced here: 68.9 us
  Pallas kernels  68.3 us (99%)
    pallas_call x1, Pallas kernels, per_device(): pl.pallas_call(functools.partial(kernel, g), out_shape=jax.ShapeDtypeStru...  66.7 us
    pallas_call x1, Pallas kernels, per_device(): pl.pallas_call(functools.partial(split_out, rows), out_shape=(jax.ShapeDt...  1.53 us

profile of v6, /device:TPU:1, one launch (start us, length us, event | category | flops | bytes accessed | tf_op | source)
XLA Modules:
  0.0 68.9 jit_solution(5404817663127789779)
XLA Ops:
  0.6 66.7 %dual_ascent.1.packed = f32[136,128]{1,0:T(8,128)} custom-call(bf16[64,256]{1,0:T(8,128)(2,1)} %bitcast.7, bf16[64,512]{1,0:T(8,128)(2,1)} %item_hbm.1, f32[128,128]{1,0:T(8,128)} %bitcast.5, f32[128,128]{1,0:T(8,128)} %bitcast.6, f32[4]{0:T(128)} %ow_hbm.1, f32[4]{0:T(128)} %ot_hbm.1, f32[4]{0:T(128)} %od_hbm.1), custom_call_target="tpu_custom_call" | custom-call | tf_op jit(solution)/shard_map/dual_ascent/pallas_call | solution.py:364
  67.4 1.5 %split_out.1 = (f32[2,128]{1,0:T(2,128)}, f32[128,128]{1,0:T(8,128)}, f32[4]{0:T(128)}) custom-call(f32[136,128]{1,0:T(8,128)} %dual_ascent.1.packed), custom_call_target="tpu_custom_call" | custom-call | tf_op jit(solution)/shard_map/split_out/pallas_call | solution.py:402
